TPU v7x, 256 devices: a whole 4x4x8 slice. The times are simulated.
256 devices in a mesh: sec: 2 (over y_hi), col: 8 (over z), row: 16 (over y_lo, x, core).
Axes of the slice: x: 4, y: 4 (y_hi: 2, y_lo: 2; y = y_hi * 2 + y_lo), z: 8, core: 2. Of those that a mesh axis runs over, the one named last changes fastest.
Arguments:
- ancestor: float32 [16384, 16384], P('row', ('sec', 'col')), may hold values from -0.3 to 0.3
- panel: float32 [2, 8192, 2048], P('sec', 'row', 'col'), may hold values from -1.5 to 1.5
- diag_inverse: float32 [2, 2048, 2048], P('sec', 'col', 'row'), may hold values from -12 to 12
- frontier: int32 [2, 16, 4], replicated, may hold values from 0 to 7, as said below
- counts: int32 [2, 16], replicated, may hold values from 1 to 4
- pattern: int32 [2, 64, 64], replicated, may hold values 0 or 1
Outputs:
- cross_block: float32 [2, 2048, 8192], P('sec', 'col', 'row')
- inverse: float32 [2, 2048, 2048], P('sec', 'col', 'row')
Inputs may be any that keep to these rules, and one draw needn't show every extreme that they name: The 4 offsets of one child and group are distinct; slot j of group g is ancestor tile 8 * g + frontier[c, g, j]. Slots j >= counts[c, g] of group g are padding for child c.
All inputs are finite; a program needn't handle non-finite values.
Results may differ from a plain program's by a relative error of at most 0.0001.
Values sent between devices are 32-bit elements; how exact they have to be, the bound alone decides.
No kernel may reach another device: no remote copies, remote signals or barrier semaphores. Data moves between devices by JAX's collectives and lax.ppermute only.
A program may use at most 128 MiB of HBM per device.

v0:
```python
import jax
import jax.numpy as jnp
from jax import lax
from jax.sharding import PartitionSpec as P

TILE = 128
GROUP = 8
SLOTS = 4


def swapped(value, axis, distance):
    mask = 2**distance
    pairs = [(source, source ^ mask) for source in range(lax.axis_size(axis))]
    return lax.ppermute(value, axis, pairs)


def from_root(value, axis, source):
    kept = jnp.where(lax.axis_index(axis) == source, value, 0).astype(value.dtype)
    return lax.psum(kept, axis)


def cut_along(value, dim, devices):
    before, after = (value.shape[:dim], value.shape[dim + 1 :])
    return jnp.moveaxis(value.reshape(*before, devices, -1, *after), dim, 0)


def summed_on_arrival(value, axis, dim):
    devices = lax.axis_size(axis)
    blocks = lax.all_to_all(cut_along(value, dim, devices), axis, 0, 0, tiled=True)
    return jnp.sum(blocks, axis=0)


def pick_tiles(
    ancestor, frontier, counts, pattern, child_id, row_start, block_start, row_groups, block_groups
):
    offsets = lax.dynamic_index_in_dim(frontier, child_id, 0, keepdims=False)
    sizes_live = lax.dynamic_index_in_dim(counts, child_id, 0, keepdims=False)
    pattern_child = lax.dynamic_index_in_dim(pattern, child_id, 0, keepdims=False)
    slot_ids = jnp.arange(SLOTS, dtype=jnp.int32)
    alive_slots = (slot_ids[None, :] < sizes_live[:, None]).astype(jnp.float32)
    within = jnp.arange(TILE, dtype=jnp.int32)
    row_offsets = lax.dynamic_slice_in_dim(offsets, row_start, row_groups, 0)
    col_offsets = lax.dynamic_slice_in_dim(offsets, block_start, block_groups, 0)
    row_tiles = (jnp.arange(row_groups, dtype=jnp.int32)[:, None] * GROUP + row_offsets).reshape(-1)
    col_tiles = (jnp.arange(block_groups, dtype=jnp.int32)[:, None] * GROUP + col_offsets).reshape(
        -1
    )
    row_indices = (row_tiles[:, None] * TILE + within[None, :]).reshape(-1)
    col_indices = (col_tiles[:, None] * TILE + within[None, :]).reshape(-1)
    picked = jnp.take(jnp.take(ancestor, row_indices, axis=0), col_indices, axis=1)
    row_alive = lax.dynamic_slice_in_dim(alive_slots, row_start, row_groups, 0).reshape(-1)
    col_alive = lax.dynamic_slice_in_dim(alive_slots, block_start, block_groups, 0).reshape(-1)
    row_slots = row_groups * SLOTS
    col_slots = block_groups * SLOTS
    pattern_block = lax.dynamic_slice(
        pattern_child, (row_start * SLOTS, block_start * SLOTS), (row_slots, col_slots)
    ).astype(jnp.float32)
    tile_mask = pattern_block * row_alive[:, None] * col_alive[None, :]
    shaped = picked.reshape(row_slots, TILE, col_slots, TILE) * tile_mask[:, None, :, None]
    return shaped.reshape(row_slots * TILE, col_slots * TILE)


def per_device(ancestor, panel, diag_inverse, frontier, counts, pattern):
    sec_index = lax.axis_index("sec")
    row_index = lax.axis_index("row")
    col_index = lax.axis_index("col")
    row_count = lax.axis_size("row")
    col_count = lax.axis_size("col")
    groups_all = frontier.shape[1]
    row_groups = groups_all // row_count
    block_groups = groups_all // (2 * col_count)
    own_block = sec_index * col_count + col_index
    row_start = row_index * row_groups
    block_start = own_block * block_groups
    mine = pick_tiles(
        ancestor,
        frontier,
        counts,
        pattern,
        sec_index,
        row_start,
        block_start,
        row_groups,
        block_groups,
    )
    theirs = pick_tiles(
        ancestor,
        frontier,
        counts,
        pattern,
        1 - sec_index,
        row_start,
        block_start,
        row_groups,
        block_groups,
    )
    partner = swapped(theirs, "sec", 0)
    leading = jnp.where(sec_index == 0, mine, partner)
    trailing = jnp.where(sec_index == 0, partner, mine)
    chosen = jnp.concatenate([leading, trailing], axis=1)
    rows_full = lax.all_gather(panel[0], "col", axis=1, tiled=True)
    starts = []
    for block_id in (col_index, col_count + col_index):
        starts.append(block_id * block_groups + 0)
    pieces = []
    for first_group in starts:
        received = from_root(rows_full, "row", first_group // row_groups)
        pieces.append(received)
    columns = jnp.concatenate(pieces, axis=0)
    cross_part = -lax.psum_scatter(
        lax.dot_general(
            columns,
            chosen,
            (((0,), (1,)), ((), ())),
            precision=lax.Precision.HIGHEST,
            preferred_element_type=jnp.float32,
        ),
        "col",
        scatter_dimension=0,
        tiled=True,
    )
    products = jnp.dot(
        cross_part, rows_full, precision=lax.Precision.HIGHEST, preferred_element_type=jnp.float32
    )
    summed = summed_on_arrival(products, "row", 1)
    inverse_part = diag_inverse[0] - summed
    return (cross_part[None], inverse_part[None])


def solution(mesh):
    return jax.shard_map(
        per_device,
        mesh=mesh,
        in_specs=(
            P("row", ("sec", "col")),
            P("sec", "row", "col"),
            P("sec", "col", "row"),
            P(),
            P(),
            P(),
        ),
        out_specs=(P("sec", "col", "row"), P("sec", "col", "row")),
        check_vma=False,
    )
```

profile of v0, /device:TPU:3, one launch (start us, length us, event | category | flops | bytes accessed | tf_op | source)
XLA Modules:
  0.0 345.1 jit_solution(13691169401568355810)
XLA Ops:
  7.2 0.0 all-gather.3.cloned.1.call-start
  7.2 0.7 all-gather.3.cloned.1.call-update
  7.9 0.0 all-reduce.3.cloned.1.call-start
  8.0 59.4 %all-gather.3.cloned.1.call-done = f32[1,512,2048]{2,1,0:T(8,128)} async-done(((f32[1,512,256]{2,1,0:T(8,128)}), f32[1,512,2048]{2,1,0:T(8,128)}) %all-gather.3.cloned.1.call-update) | async-done | bytes 4194320 | tf_op jit(solution)/shard_map/all_gather | solution.py:101
  67.3 6.8 %bitcast_select_fusion.1 = (f32[512,2048]{1,0:T(8,128)}, f32[512,2048]{1,0:T(8,128)}) fusion(f32[1,512,2048]{2,1,0:T(8,128)} %all-gather.3.cloned.1.call-done, pred[]{:T(512)S(6)} %eq.10, pred[]{:T(512)S(6)} %eq.11), kind=kLoop, calls=%fused_computation.11 | loop fusion | flops 2097152 | bytes 12582914 | tf_op jit(solution)/shard_map/jit(_where)/select_n | solution.py:18
  74.1 0.0 copy-start.3
  74.1 0.0 copy-start.2
  74.1 0.0 all-reduce.3.cloned.1.call-update
  74.1 0.0 reduce-scatter.2.cloned.1.call-start
  74.2 0.6 copy-done.3
  74.8 0.1 fusion.13
  74.9 0.8 fusion.24
  75.7 0.1 copy.15
  75.8 0.0 copy-done.2
  75.8 0.2 fusion.18
  76.0 0.1 compare_select_fusion
  76.1 5.0 %gather_fusion.2 = f32[512,1024]{1,0:T(8,128)S(1)} fusion(f32[1024,1024]{1,0:T(8,128)} %param.10, s32[1024]{0:T(1024)S(1)} %pad_clamp_fusion.1), kind=kCustom, calls=%fused_computation.2.clone | custom fusion | bytes 4196352 | tf_op jit(solution)/shard_map/jit(_take)/gather | solution.py:50
  81.1 0.1 compare_and_fusion
  81.2 1.5 broadcast_select_fusion
  82.7 1.9 copy.14
  84.7 1.6 gather_fusion.3
  86.3 0.2 mul.159
  86.5 1.2 bitcast_multiply_fusion
  87.7 2.7 collective-permute-start
  90.4 0.1 copy.13
  90.5 0.1 compare_select_fusion.2
  90.6 5.1 %gather_fusion = f32[512,1024]{1,0:T(8,128)S(1)} fusion(f32[1024,1024]{1,0:T(8,128)} %param.10, s32[1024]{0:T(1024)S(1)} %pad_clamp_fusion.3), kind=kCustom, calls=%fused_computation.clone | custom fusion | bytes 4196352 | tf_op jit(solution)/shard_map/jit(_take)/gather | solution.py:50
  95.7 0.1 compare_and_fusion.2
  95.8 1.5 broadcast_select_fusion.1
  97.3 1.9 copy.12
  99.3 1.6 gather_fusion.1
  100.9 12.5 %collective-permute-done = f32[512,512]{0,1:T(8,128)} collective-permute-done((f32[512,512]{0,1:T(8,128)}, f32[512,512]{0,1:T(8,128)}, u32[]{:S(2)}, u32[]{:S(2)}) %collective-permute-start) | collective-permute-done | bytes 1048608 | tf_op jit(solution)/shard_map/ppermute | solution.py:14
  113.4 0.2 mul.146
  113.6 1.5 broadcast_select_fusion.3
  115.1 103.7 %all-reduce.3.cloned.1.call-done = (f32[512,2048]{1,0:T(8,128)}, f32[512,2048]{1,0:T(8,128)}) async-done(((f32[512,2048]{1,0:T(8,128)}, f32[512,2048]{1,0:T(8,128)}), (f32[512,2048]{1,0:T(8,128)}, f32[512,2048]{1,0:T(8,128)})) %all-reduce.3.cloned.1.call-update) | async-done | bytes 8388624 | tf_op jit(solution)/shard_map/psum | solution.py:19
  218.8 16.6 %fusion = f32[2048,512]{1,0:T(8,128)} fusion(f32[512,2048]{1,0:T(8,128)} %get-tuple-element.8, f32[512,2048]{1,0:T(8,128)} %get-tuple-element.9, f32[512,512]{0,1:T(8,128)S(1)} %get-tuple-element.13, f32[512,512]{0,1:T(8,128)S(1)} %get-tuple-element.12), kind=kOutput, calls=%fused_computation.4 | convolution fusion | flops 12887523328 | bytes 14680064 | tf_op jit(solution)/shard_map/dot_general | solution.py:111
  235.4 0.0 reduce-scatter.2.cloned.1.call-update
  235.4 60.8 %reduce-scatter.2.cloned.1.call-done = f32[256,512]{1,0:T(8,128)} async-done(((f32[2048,512]{1,0:T(8,128)}), f32[256,512]{1,0:T(8,128)}) %reduce-scatter.2.cloned.1.call-update) | async-done | bytes 524304 | tf_op jit(solution)/shard_map/reduce_scatter | solution.py:110
  296.1 5.5 %fusion.9 = f32[32,16,8,128]{3,2,1,0:T(8,128)S(1)} fusion(f32[1,512,2048]{2,1,0:T(8,128)} %all-gather.3.cloned.1.call-done, f32[256,512]{1,0:T(8,128)} %reduce-scatter.2.cloned.1.call-done), kind=kOutput, calls=%fused_computation.16 | convolution fusion | flops 3221356544 | bytes 6815744 | tf_op jit(solution)/shard_map/dot_general | solution.py:122
  301.7 1.6 copy.27
  303.2 0.0 copy-start
  303.2 6.2 %all-to-all-start = ((f32[16,256,128]{2,1,0:T(8,128)}), f32[16,256,128]{2,1,0:T(8,128)S(1)}, u32[]{:S(2)}, u32[]{:S(2)}) async-start(f32[16,256,128]{2,1,0:T(8,128)} %bitcast.79), calls=%async_computation.1 | async-start | bytes 4194304 | tf_op jit(solution)/shard_map/all_to_all | solution.py:29
  309.5 0.0 copy-done
  309.5 0.0 copy-start.1
  309.5 0.8 negate_bitcast_fusion
  310.3 27.5 %all-to-all-done = f32[16,256,128]{2,1,0:T(8,128)S(1)} async-done(((f32[16,256,128]{2,1,0:T(8,128)}), f32[16,256,128]{2,1,0:T(8,128)S(1)}, u32[]{:S(2)}, u32[]{:S(2)}) %all-to-all-start) | async-done | bytes 2097184 | tf_op jit(solution)/shard_map/all_to_all | solution.py:29
  337.8 0.1 reduce_sum.11
  337.9 0.0 copy-done.1
  337.9 0.7 bitcast_subtract_fusion
  (7 shorter events, 0.1 us)
Async XLA Ops:
  7.2 60.2 %all-gather.3.cloned.1.call-start = ((), (), s32[]{:S(2)}) async-start(), calls=%async_computation.3 | async-start | bytes 4718592 | tf_op jit(solution)/shard_map/all_gather | solution.py:101
  7.9 210.9 %all-reduce.3.cloned.1.call-start = ((), (), s32[]{:S(2)}) async-start(), calls=%async_computation.4 | async-start | bytes 16777216 | tf_op jit(solution)/shard_map/psum | solution.py:19
  74.1 0.7 copy-start.3
  74.1 1.7 copy-start.2
  74.1 222.0 %reduce-scatter.2.cloned.1.call-start = ((), (), s32[]{:S(2)}) async-start(), calls=%async_computation.2 | async-start | bytes 4718592 | tf_op jit(solution)/shard_map/reduce_scatter | solution.py:110
  87.7 25.7 %collective-permute-start = (f32[512,512]{0,1:T(8,128)}, f32[512,512]{0,1:T(8,128)}, u32[]{:S(2)}, u32[]{:S(2)}) collective-permute-start(f32[512,512]{0,1:T(8,128)} %bitcast_multiply_fusion), channel_id=1, source_target_pairs={{0,128},{128,0},{1,129},{129,1},{2,130},{130,2},{3,131},{131,3},{4... | collective-permute-start | bytes 3145736 | tf_op jit(solution)/shard_map/ppermute | solution.py:14
  303.2 6.2 %copy-start = (f32[256,512]{1,0:T(8,128)S(1)}, f32[256,512]{1,0:T(8,128)}, u32[]{:S(2)}) copy-start(f32[256,512]{1,0:T(8,128)} %reduce-scatter.2.cloned.1.call-done) | copy-start | bytes 1572868
  303.2 34.6 %all-to-all-start = ((f32[16,256,128]{2,1,0:T(8,128)}), f32[16,256,128]{2,1,0:T(8,128)S(1)}, u32[]{:S(2)}, u32[]{:S(2)}) async-start(f32[16,256,128]{2,1,0:T(8,128)} %bitcast.79), calls=%async_computation.1 | async-start | bytes 4194304 | tf_op jit(solution)/shard_map/all_to_all | solution.py:29
  309.5 28.5 %copy-start.1 = (f32[1,256,128]{2,1,0:T(8,128)S(1)}, f32[1,256,128]{2,1,0:T(8,128)}, u32[]{:S(2)}) copy-start(f32[1,256,128]{2,1,0:T(8,128)} %param.12) | copy-start | bytes 393220
Sparse Core Ops, SparseCore 0:
  9.8 57.5 all-gather.2
  74.3 144.4 all-reduce.2
  235.5 60.5 reduce-scatter.1
where the time goes:
time: 346 us; the launch traced here: 345 us
  waiting for transfers between devices  265 us (77%)
  matrix products  22.1 us (6%)
  local copies, waits for them, and re-layouts  20 us (6%)
  other arithmetic  15.5 us (4%)
  between operations  13.9 us (4%)
  starting transfers between devices  9.09 us (3%)
    psum x1, waiting for transfers between devices, from_root(): return lax.psum(kept, axis)  104 us
    reduce_scatter x1, waiting for transfers between devices, per_device(): lax.psum_scatter(lax.dot_general(columns, chosen, (((0,), (1,)), ((), ())...  60.8 us
    all_gather x1, waiting for transfers between devices, per_device(): rows_full = lax.all_gather(panel[0], 'col', axis=1, tiled=True)  59.4 us
    all_to_all x1, waiting for transfers between devices, summed_on_arrival(): lax.all_to_all(cut_along(value, dim, devices), axis, 0, 0, tiled=True)  27.5 us
    dot_general x1, matrix products, per_device(): lax.dot_general(columns, chosen, (((0,), (1,)), ((), ())), precision=lax....  16.6 us
    ppermute x1, waiting for transfers between devices, swapped(): return lax.ppermute(value, axis, pairs)  12.5 us
    gather x2, local copies, waits for them, and re-layouts, pick_tiles(): jnp.take(ancestor, row_indices, axis=0)  10.1 us
  transfers between devices with their start and end apart: 5, of which 5 were waited for; matrix products, arithmetic and copies ran while one was open for 7% of the time, Pallas kernels for 0%

commit v1 on v0

--- a/solution.py
+++ b/solution.py
@@ -98,7 +98,9 @@
     leading = jnp.where(sec_index == 0, mine, partner)
     trailing = jnp.where(sec_index == 0, partner, mine)
     chosen = jnp.concatenate([leading, trailing], axis=1)
-    rows_full = lax.all_gather(panel[0], "col", axis=1, tiled=True)
+    block = panel[0]
+    sent = jnp.stack([block] * lax.axis_size("col"))
+    rows_full = jnp.concatenate(lax.all_to_all(sent, "col", 0, 0), axis=1)
     starts = []
     for block_id in (col_index, col_count + col_index):
         starts.append(block_id * block_groups + 0)

time: 346 us -> 391 us (1.13)
  waiting for transfers between devices: 265 us -> 298 us
  starting transfers between devices: 9.09 us -> 17.4 us
    all_to_all x0 -> x1, waiting for transfers between devices: none -> 96.8 us  [per_device(): rows_full = jnp.concatenate(lax.all_to_all(sent, 'col', 0, 0), axis=1)]
    all_gather x1 -> x0, waiting for transfers between devices: 59.4 us -> none  [per_device(): rows_full = lax.all_gather(panel[0], 'col', axis=1, tiled=True)]
    all_to_all x0 -> x1, starting transfers between devices: none -> 8.19 us  [per_device(): rows_full = jnp.concatenate(lax.all_to_all(sent, 'col', 0, 0), axis=1)]
where the time goes in v1:
time: 391 us
  waiting for transfers between devices  298 us (76%)
  matrix products  23.2 us (6%)
  local copies, waits for them, and re-layouts  22.1 us (6%)
  starting transfers between devices  17.4 us (4%)
  other arithmetic  15.5 us (4%)
  between operations  14.2 us (4%)
    psum x1, waiting for transfers between devices, from_root(): return lax.psum(kept, axis)  100 us
    all_to_all x1, waiting for transfers between devices, per_device(): rows_full = jnp.concatenate(lax.all_to_all(sent, 'col', 0, 0), axis=1)  96.8 us
    reduce_scatter x1, waiting for transfers between devices, per_device(): lax.psum_scatter(lax.dot_general(columns, chosen, (((0,), (1,)), ((), ())...  60.8 us
    all_to_all x1, waiting for transfers between devices, summed_on_arrival(): lax.all_to_all(cut_along(value, dim, devices), axis, 0, 0, tiled=True)  27.5 us
    dot_general x1, matrix products, per_device(): lax.dot_general(columns, chosen, (((0,), (1,)), ((), ())), precision=lax....  16.6 us
    ppermute x1, waiting for transfers between devices, swapped(): return lax.ppermute(value, axis, pairs)  12.7 us
    gather x2, local copies, waits for them, and re-layouts, pick_tiles(): jnp.take(ancestor, row_indices, axis=0)  10 us
    all_to_all x1, starting transfers between devices, per_device(): rows_full = jnp.concatenate(lax.all_to_all(sent, 'col', 0, 0), axis=1)  8.19 us
  transfers between devices with their start and end apart: 5, of which 5 were waited for; matrix products, arithmetic and copies ran while one was open for 7% of the time, Pallas kernels for 0%

profile of v1, /device:TPU:3, one launch (start us, length us, event | category | flops | bytes accessed | tf_op | source)
XLA Modules:
  0.0 390.5 jit_solution(15972735812021151962)
XLA Ops:
  7.2 1.2 copy.8
  8.4 2.5 stack.3
  10.9 8.2 %all-to-all-start = ((f32[8,512,256]{1,2,0:T(8,128)}), f32[8,512,256]{1,2,0:T(8,128)}, u32[]{:S(2)}, u32[]{:S(2)}) async-start(f32[8,512,256]{1,2,0:T(8,128)} %stack.3), calls=%async_computation | async-start | bytes 8388608 | tf_op jit(solution)/shard_map/all_to_all | solution.py:103
  19.1 0.0 all-reduce.3.cloned.1.call-start
  19.2 96.8 %all-to-all-done = f32[8,512,256]{1,2,0:T(8,128)} async-done(((f32[8,512,256]{1,2,0:T(8,128)}), f32[8,512,256]{1,2,0:T(8,128)}, u32[]{:S(2)}, u32[]{:S(2)}) %all-to-all-start) | async-done | bytes 4194336 | tf_op jit(solution)/shard_map/all_to_all | solution.py:103
  116.0 6.7 %bitcast_select_fusion.1 = (f32[512,2048]{0,1:T(8,128)}, f32[512,2048]{0,1:T(8,128)}) fusion(f32[8,512,256]{1,2,0:T(8,128)} %all-to-all-done, pred[]{:T(512)S(6)} %eq.10, pred[]{:T(512)S(6)} %eq.11), kind=kLoop, calls=%fused_computation.9 | loop fusion | flops 2097152 | bytes 12582914 | tf_op jit(solution)/shard_map/jit(_where)/select_n | solution.py:18
  122.7 0.0 copy-start.3
  122.7 0.0 copy-start.2
  122.7 0.0 all-reduce.3.cloned.1.call-update
  122.7 0.0 reduce-scatter.2.cloned.1.call-start
  122.8 0.6 copy-done.3
  123.4 0.1 fusion.9
  123.5 0.8 fusion.20
  124.3 0.1 copy.12
  124.4 0.0 copy-done.2
  124.4 0.2 fusion.14
  124.6 0.1 compare_select_fusion
  124.7 5.0 %gather_fusion.2 = f32[512,1024]{1,0:T(8,128)S(1)} fusion(f32[1024,1024]{1,0:T(8,128)} %param.10, s32[1024]{0:T(1024)S(1)} %pad_clamp_fusion.1), kind=kCustom, calls=%fused_computation.2.clone | custom fusion | bytes 4196352 | tf_op jit(solution)/shard_map/jit(_take)/gather | solution.py:50
  129.7 0.1 compare_and_fusion
  129.8 1.5 broadcast_select_fusion
  131.3 1.9 copy.11
  133.3 1.6 gather_fusion.3
  134.9 0.2 mul.159
  135.1 1.2 bitcast_multiply_fusion
  136.3 2.9 collective-permute-start
  139.2 0.1 copy.10
  139.3 0.1 compare_select_fusion.2
  139.4 5.0 %gather_fusion = f32[512,1024]{1,0:T(8,128)S(1)} fusion(f32[1024,1024]{1,0:T(8,128)} %param.10, s32[1024]{0:T(1024)S(1)} %pad_clamp_fusion.3), kind=kCustom, calls=%fused_computation.clone | custom fusion | bytes 4196352 | tf_op jit(solution)/shard_map/jit(_take)/gather | solution.py:50
  144.4 0.1 compare_and_fusion.2
  144.5 1.5 broadcast_select_fusion.1
  146.0 1.9 copy.9
  148.0 1.6 gather_fusion.1
  149.6 12.7 %collective-permute-done = f32[512,512]{0,1:T(8,128)} collective-permute-done((f32[512,512]{0,1:T(8,128)}, f32[512,512]{0,1:T(8,128)}, u32[]{:S(2)}, u32[]{:S(2)}) %collective-permute-start) | collective-permute-done | bytes 1048608 | tf_op jit(solution)/shard_map/ppermute | solution.py:14
  162.3 0.2 mul.146
  162.5 1.5 broadcast_select_fusion.3
  164.0 100.3 %all-reduce.3.cloned.1.call-done = (f32[512,2048]{0,1:T(8,128)}, f32[512,2048]{0,1:T(8,128)}) async-done(((f32[512,2048]{0,1:T(8,128)}, f32[512,2048]{0,1:T(8,128)}), (f32[512,2048]{0,1:T(8,128)}, f32[512,2048]{0,1:T(8,128)})) %all-reduce.3.cloned.1.call-update) | async-done | bytes 8388624 | tf_op jit(solution)/shard_map/psum | solution.py:19
  264.3 16.6 %fusion = f32[2048,512]{1,0:T(8,128)} fusion(f32[512,2048]{0,1:T(8,128)} %get-tuple-element.8, f32[512,2048]{0,1:T(8,128)} %get-tuple-element.9, f32[512,512]{0,1:T(8,128)S(1)} %get-tuple-element.13, f32[512,512]{0,1:T(8,128)S(1)} %get-tuple-element.12), kind=kOutput, calls=%fused_computation.4 | convolution fusion | flops 12887523328 | bytes 14680064 | tf_op jit(solution)/shard_map/dot_general | solution.py:113
  281.0 0.0 reduce-scatter.2.cloned.1.call-update
  281.0 60.8 %reduce-scatter.2.cloned.1.call-done = f32[256,512]{1,0:T(8,128)} async-done(((f32[2048,512]{1,0:T(8,128)}), f32[256,512]{1,0:T(8,128)}) %reduce-scatter.2.cloned.1.call-update) | async-done | bytes 524304 | tf_op jit(solution)/shard_map/reduce_scatter | solution.py:112
  341.8 6.6 %convolution_bitcast_fusion = f32[16,256,128]{2,1,0:T(8,128)} fusion(f32[16,128,512]{2,1,0:T(8,128)} %bitcast.21, f32[256,512]{1,0:T(8,128)} %reduce-scatter.2.cloned.1.call-done), kind=kOutput, calls=%fused_computation.13 | convolution fusion | flops 3221356544 | bytes 6815744 | tf_op jit(solution)/shard_map/dot_general | solution.py:124
  348.3 0.0 copy-start
  348.3 6.2 %all-to-all-start.1 = ((f32[16,256,128]{2,1,0:T(8,128)}), f32[16,256,128]{2,1,0:T(8,128)S(1)}, u32[]{:S(2)}, u32[]{:S(2)}) async-start(f32[16,256,128]{2,1,0:T(8,128)} %convolution_bitcast_fusion), calls=%async_computation.2 | async-start | bytes 4194304 | tf_op jit(solution)/shard_map/all_to_all | solution.py:29
  354.6 0.0 copy-done
  354.6 0.0 copy-start.1
  354.6 0.8 negate_bitcast_fusion
  355.4 27.5 %all-to-all-done.1 = f32[16,256,128]{2,1,0:T(8,128)S(1)} async-done(((f32[16,256,128]{2,1,0:T(8,128)}), f32[16,256,128]{2,1,0:T(8,128)S(1)}, u32[]{:S(2)}, u32[]{:S(2)}) %all-to-all-start.1) | async-done | bytes 2097184 | tf_op jit(solution)/shard_map/all_to_all | solution.py:29
  382.9 0.1 reduce_sum.11
  383.0 0.0 copy-done.1
  383.0 0.7 bitcast_subtract_fusion
  (7 shorter events, 0.1 us)
Async XLA Ops:
  10.9 105.0 %all-to-all-start = ((f32[8,512,256]{1,2,0:T(8,128)}), f32[8,512,256]{1,2,0:T(8,128)}, u32[]{:S(2)}, u32[]{:S(2)}) async-start(f32[8,512,256]{1,2,0:T(8,128)} %stack.3), calls=%async_computation | async-start | bytes 8388608 | tf_op jit(solution)/shard_map/all_to_all | solution.py:103
  19.1 245.2 %all-reduce.3.cloned.1.call-start = ((), (), s32[]{:S(2)}) async-start(), calls=%async_computation.4 | async-start | bytes 16777216 | tf_op jit(solution)/shard_map/psum | solution.py:19
  122.7 0.7 copy-start.3
  122.7 1.7 copy-start.2
  122.7 219.1 %reduce-scatter.2.cloned.1.call-start = ((), (), s32[]{:S(2)}) async-start(), calls=%async_computation.3 | async-start | bytes 4718592 | tf_op jit(solution)/shard_map/reduce_scatter | solution.py:112
  136.3 26.1 %collective-permute-start = (f32[512,512]{0,1:T(8,128)}, f32[512,512]{0,1:T(8,128)}, u32[]{:S(2)}, u32[]{:S(2)}) collective-permute-start(f32[512,512]{0,1:T(8,128)} %bitcast_multiply_fusion), channel_id=1, source_target_pairs={{0,128},{128,0},{1,129},{129,1},{2,130},{130,2},{3,131},{131,3},{4... | collective-permute-start | bytes 3145736 | tf_op jit(solution)/shard_map/ppermute | solution.py:14
  348.3 6.2 %copy-start = (f32[256,512]{1,0:T(8,128)S(1)}, f32[256,512]{1,0:T(8,128)}, u32[]{:S(2)}) copy-start(f32[256,512]{1,0:T(8,128)} %reduce-scatter.2.cloned.1.call-done) | copy-start | bytes 1572868
  348.3 34.6 %all-to-all-start.1 = ((f32[16,256,128]{2,1,0:T(8,128)}), f32[16,256,128]{2,1,0:T(8,128)S(1)}, u32[]{:S(2)}, u32[]{:S(2)}) async-start(f32[16,256,128]{2,1,0:T(8,128)} %convolution_bitcast_fusion), calls=%async_computation.2 | async-start | bytes 4194304 | tf_op jit(solution)/shard_map/all_to_all | solution.py:29
  354.6 28.5 %copy-start.1 = (f32[1,256,128]{2,1,0:T(8,128)S(1)}, f32[1,256,128]{2,1,0:T(8,128)}, u32[]{:S(2)}) copy-start(f32[1,256,128]{2,1,0:T(8,128)} %param.12) | copy-start | bytes 393220
Sparse Core Ops, SparseCore 0:
  122.8 141.4 all-reduce.2
  281.1 60.5 reduce-scatter.1
